TPU v7x, 32 devices: a whole 2x2x4 slice. The times are simulated.
32 devices in a mesh: groups: 2 (over x), ctx: 8 (over z, y), exp: 2 (over core).
Axes of the slice: x: 2, y: 2, z: 4, core: 2. Of those that a mesh axis runs over, the one named last changes fastest.
Arguments:
- tokens: bfloat16 [2048, 5120], P(('groups', 'ctx'), 'exp'), parts along dimension 0, may hold values from -6 to 6
- route_ids: int32 [2048, 2], P(('groups', 'ctx')), parts along dimension 0, may hold values from 0 to 3, all different within a row; in each aligned block of 128 rows (0 to 127, 128 to 255, ...) at most 128 rows name the same one
- route_gates: float32 [2048, 2], P(('groups', 'ctx')), parts along dimension 0, may hold values from 0.2 to 1
- w_in: bfloat16 [8, 5120, 1536], P('ctx', 'exp'), may hold values from -0.078125 to 0.078125
- w_out: bfloat16 [8, 768, 5120], P('ctx', None, 'exp'), may hold values from -0.15625 to 0.15625
Outputs:
- mixed: bfloat16 [2048, 5120], P(('groups', 'ctx'), 'exp'), parts along dimension 0
There are 2 independent parts, one for each index of `groups`. A program takes and returns all parts, laid end to end along the dimension named above; an argument that names none is the same for every part. Nothing has to cross between parts.
Inputs may be any that keep to these rules, and one draw needn't show every extreme that they name: `route_ids`: within the 128 rows of one device no expert is named more than 128 times, a bound that some block reaches; the ids of one token differ.
All inputs are finite; a program needn't handle non-finite values.
Results may differ from a plain program's by a relative error of at most 0.025.
Values may be sent and summed in bfloat16 or wider, within the bound.
A program may use at most 64 MiB of HBM per device.

v0:
```python
import jax
import jax.numpy as jnp
from jax import lax
from jax.sharding import PartitionSpec as P


def expert_half(rows, w_in, w_out):
    gate_up = jnp.dot(rows, w_in[0], preferred_element_type=jnp.float32)
    summed = lax.psum(gate_up.astype(jnp.bfloat16), "exp").astype(jnp.float32)
    hidden_units = w_out.shape[1]
    hidden = (jax.nn.silu(summed[:, :hidden_units]) * summed[:, hidden_units:]).astype(jnp.bfloat16)
    return jnp.dot(hidden, w_out[0], preferred_element_type=jnp.float32).astype(jnp.bfloat16)


def gate_table(route_ids, route_gates, experts):
    named = route_ids[:, :, None] == jnp.arange(experts, dtype=jnp.int32)
    return jnp.sum(jnp.where(named, route_gates[:, :, None], 0.0), axis=1)


def dense(tokens, route_ids, route_gates, w_in, w_out):
    experts = lax.axis_size("ctx") // 2
    gates = lax.all_gather(gate_table(route_ids, route_gates, experts), "ctx", axis=0, tiled=True)
    gate = lax.dynamic_slice_in_dim(gates, lax.axis_index("ctx") // 2, 1, axis=1)
    rows = lax.all_gather(tokens, "ctx", axis=0, tiled=True)
    out = (expert_half(rows, w_in, w_out).astype(jnp.float32) * gate).astype(jnp.bfloat16)
    return lax.psum_scatter(out, "ctx", scatter_dimension=0, tiled=True)


def per_device(tokens, route_ids, route_gates, w_in, w_out):
    ctx_size = lax.axis_size("ctx")
    experts = ctx_size // 2
    tok_rows, half_width = tokens.shape
    top_count = route_ids.shape[1]
    capacity = 2 * ((top_count * tok_rows + experts - 1) // experts)
    if capacity >= tok_rows:
        return dense(tokens, route_ids, route_gates, w_in, w_out)
    slots = experts * capacity
    flat_ids = route_ids.reshape(-1)
    onehot = (flat_ids[:, None] == jnp.arange(experts, dtype=jnp.int32)[None, :]).astype(jnp.int32)
    before = jnp.cumsum(onehot, axis=0) - onehot
    rank = jnp.sum(before * onehot, axis=1)
    slot_of = flat_ids * capacity + rank
    placed = (slot_of[:, None] == jnp.arange(slots, dtype=jnp.int32)[None, :]).astype(jnp.bfloat16)
    placed = placed.reshape(tok_rows, top_count, slots)
    every_map = jnp.sum(placed.astype(jnp.float32), axis=1).astype(jnp.bfloat16)
    gathered = lax.dot_general(
        every_map, tokens, (((0,), (0,)), ((), ())), preferred_element_type=jnp.float32
    ).astype(jnp.bfloat16)
    outgoing = jnp.broadcast_to(
        gathered.reshape(experts, 1, capacity, half_width), (experts, 2, capacity, half_width)
    ).reshape(ctx_size, capacity, half_width)
    received = lax.all_to_all(outgoing, "ctx", split_axis=0, concat_axis=0, tiled=True)
    count = received.shape[1]
    partial_out = expert_half(received.reshape(-1, half_width), w_in, w_out).reshape(
        ctx_size, count, half_width
    )
    returned = lax.all_to_all(partial_out, "ctx", split_axis=0, concat_axis=0, tiled=True)
    results = (
        jnp.sum(returned.astype(jnp.float32).reshape(experts, 2, capacity, half_width), axis=1)
        .astype(jnp.bfloat16)
        .reshape(slots, half_width)
    )
    mixed = jnp.zeros((tok_rows, half_width), jnp.float32)
    for route in range(top_count):
        route_out = jnp.dot(placed[:, route], results, preferred_element_type=jnp.float32)
        mixed = mixed + route_gates[:, route : route + 1] * route_out
    return mixed.astype(jnp.bfloat16)


def solution(mesh):
    placed = (
        P(("groups", "ctx"), "exp"),
        P(("groups", "ctx"), None),
        P(("groups", "ctx"), None),
        P("ctx", "exp", None),
        P("ctx", None, "exp"),
    )
    return jax.shard_map(
        per_device,
        mesh=mesh,
        in_specs=placed,
        out_specs=P(("groups", "ctx"), "exp"),
        check_vma=False,
    )
```

profile of v0, /device:TPU:0, one launch (start us, length us, event | category | flops | bytes accessed | tf_op | source)
XLA Modules:
  0.0 253.9 jit_solution(14668510302520521451)
XLA Ops:
  6.5 0.0 all-gather.2.cloned.1.call-start
  6.5 0.7 all-gather.2.cloned.1.call-update
  7.3 0.0 copy-start
  7.3 0.0 copy-start.1
  7.3 0.0 all-reduce.2.cloned.1.call-start
  7.3 90.8 %all-gather.2.cloned.1.call-done = bf16[1024,2560]{1,0:T(8,128)(2,1)} async-done(((bf16[128,2560]{1,0:T(8,128)(2,1)}), bf16[1024,2560]{1,0:T(8,128)(2,1)}) %all-gather.2.cloned.1.call-update) | async-done | bytes 5242896 | tf_op jit(solution)/shard_map/all_gather | solution.py:24
  98.2 13.3 %fusion.3 = bf16[1024,1536]{1,0:T(8,128)(2,1)} fusion(bf16[1024,2560]{1,0:T(8,128)(2,1)} %all-gather.2.cloned.1.call-done, bf16[1,2560,1536]{2,1,0:T(8,128)(2,1)} %param.8), kind=kOutput, calls=%fused_computation.5 | convolution fusion | flops 8054636544 | bytes 16252928 | tf_op jit(solution)/shard_map/dot_general | solution.py:8
  111.5 0.0 all-reduce.2.cloned.1.call-update
  111.5 0.0 reduce-scatter.2.cloned.1.call-start
  111.6 0.0 copy-done
  111.6 0.0 copy-done.1
  111.6 26.1 %all_gather.7 = f32[1024,4]{0,1:T(4,128)S(1)} all-gather(f32[128,4]{0,1:T(4,128)S(1)} %select_reduce_fusion), channel_id=1, replica_groups=mesh['groups'=2,'ctx'=8,'exp'=2] {'ctx'}, dimensions={0}, use_global_device_ids=true | all-gather | bytes 18432 | tf_op jit(solution)/shard_map/all_gather | solution.py:22
  137.7 0.0 all-reduce.2.cloned.1.call-done
  137.8 0.0 copy-start.2
  137.8 2.9 %convert_element_type.19 = f32[1024,1536]{1,0:T(8,128)S(1)} convert(bf16[1024,1536]{1,0:T(8,128)(2,1)} %all-reduce.2.cloned.1.call-done) | non-fusion elementwise | flops 1572864 | bytes 9437184 | tf_op jit(solution)/shard_map/convert_element_type | solution.py:9
  140.7 0.1 copy-done.2
  140.8 6.1 %multiply_convert_fusion = bf16[1024,2560]{1,0:T(8,128)(2,1)} fusion(f32[1024]{0:T(1024)S(1)} %bitcast.10, bf16[1,768,2560]{2,1,0:T(8,128)(2,1)S(1)} %copy-done.2, f32[1024,1536]{1,0:T(8,128)S(1)} %convert_element_type.19), kind=kOutput, calls=%fused_computation | convolution fusion | flops 4041736192 | bytes 15470592 | tf_op jit(solution)/shard_map/dot_general | solution.py:12
  146.9 0.0 reduce-scatter.2.cloned.1.call-update
  146.9 100.4 %reduce-scatter.2.cloned.1.call-done = bf16[128,2560]{1,0:T(8,128)(2,1)} async-done(((bf16[1024,2560]{1,0:T(8,128)(2,1)}), bf16[128,2560]{1,0:T(8,128)(2,1)}) %reduce-scatter.2.cloned.1.call-update) | async-done | bytes 655376 | tf_op jit(solution)/shard_map/reduce_scatter | solution.py:26
  (2 shorter events, 0.0 us)
Async XLA Ops:
  6.5 91.6 %all-gather.2.cloned.1.call-start = ((), (), s32[]{:S(2)}) async-start(), calls=%async_computation.1 | async-start | bytes 5898240 | tf_op jit(solution)/shard_map/all_gather | solution.py:24
  7.3 104.3 %copy-start = (f32[128,2]{0,1:T(2,128)S(1)}, f32[128,2]{0,1:T(2,128)}, u32[]{:S(2)}) copy-start(f32[128,2]{0,1:T(2,128)} %param.7) | copy-start | bytes 3076
  7.3 104.3 %copy-start.1 = (s32[128,2]{0,1:T(2,128)S(1)}, s32[128,2]{0,1:T(2,128)}, u32[]{:S(2)}) copy-start(s32[128,2]{0,1:T(2,128)} %param.6) | copy-start | bytes 3076
  7.3 130.5 %all-reduce.2.cloned.1.call-start = ((), (), s32[]{:S(2)}) async-start(), calls=%async_computation.2 | async-start | bytes 6291456 | tf_op jit(solution)/shard_map/psum | solution.py:9
  111.5 135.9 %reduce-scatter.2.cloned.1.call-start = ((), (), s32[]{:S(2)}) async-start(), calls=%async_computation.3 | async-start | bytes 5898240 | tf_op jit(solution)/shard_map/reduce_scatter | solution.py:26
  137.8 3.1 %copy-start.2 = (bf16[1,768,2560]{2,1,0:T(8,128)(2,1)S(1)}, bf16[1,768,2560]{2,1,0:T(8,128)(2,1)}, u32[]{:S(2)}) copy-start(bf16[1,768,2560]{2,1,0:T(8,128)(2,1)} %param.9) | copy-start | bytes 11796484
Sparse Core Ops, SparseCore 0:
  9.5 88.5 all-gather.1
  111.6 21.4 all-reduce.1
  147.1 100.2 reduce-scatter.1
where the time goes:
time: 254 us
  waiting for transfers between devices  192 us (76%)
  blocking collectives  26.1 us (10%)
  matrix products  19.4 us (8%)
  between operations  13.2 us (5%)
  other arithmetic  2.91 us (1%)
    reduce_scatter x1, waiting for transfers between devices, dense(): return lax.psum_scatter(out, 'ctx', scatter_dimension=0, tiled=True)  100 us
    all_gather x1, waiting for transfers between devices, dense(): rows = lax.all_gather(tokens, 'ctx', axis=0, tiled=True)  90.8 us
    all_gather x1, blocking collectives, dense(): lax.all_gather(gate_table(route_ids, route_gates, experts), 'ctx', axis=0...  26.1 us
    dot_general x1, matrix products, expert_half(): gate_up = jnp.dot(rows, w_in[0], preferred_element_type=jnp.float32)  13.3 us
    dot_general x1, matrix products, expert_half(): jnp.dot(hidden, w_out[0], preferred_element_type=jnp.float32)  6.08 us
  transfers between devices with their start and end apart: 3, of which 2 were waited for; matrix products, arithmetic and copies ran while one was open for 0% of the time, Pallas kernels for 0%

commit v1 on v0

--- a/solution.py
+++ b/solution.py
@@ -19,7 +19,15 @@
 
 def dense(tokens, route_ids, route_gates, w_in, w_out):
     experts = lax.axis_size("ctx") // 2
-    gates = lax.all_gather(gate_table(route_ids, route_gates, experts), "ctx", axis=0, tiled=True)
+    gates = jnp.concatenate(
+        lax.all_to_all(
+            jnp.stack([gate_table(route_ids, route_gates, experts)] * lax.axis_size("ctx")),
+            "ctx",
+            0,
+            0,
+        ),
+        axis=0,
+    )
     gate = lax.dynamic_slice_in_dim(gates, lax.axis_index("ctx") // 2, 1, axis=1)
     rows = lax.all_gather(tokens, "ctx", axis=0, tiled=True)
     out = (expert_half(rows, w_in, w_out).astype(jnp.float32) * gate).astype(jnp.bfloat16)

time: 254 us -> 253 us (level)
  blocking collectives: 26.1 us -> 0 us
  waiting for transfers between devices: 192 us -> 213 us
  starting transfers between devices: 0.08 us -> 3.42 us
    all_gather x1 -> x0, blocking collectives: 26.1 us -> none  [dense(): lax.all_gather(gate_table(route_ids, route_gates, experts), 'ctx', axis=0...]
    psum x1, waiting for transfers between devices: 0.02 us -> 11.1 us  [expert_half(): summed = lax.psum(gate_up.astype(jnp.bfloat16), 'exp').astype(jnp.float32)]
    all_to_all x0 -> x1, waiting for transfers between devices: none -> 6.45 us  [dense(): lax.all_to_all(jnp.stack([gate_table(route_ids, route_gates, experts)] *...]
    reduce_scatter x1, waiting for transfers between devices: 100 us -> 104 us  [dense(): return lax.psum_scatter(out, 'ctx', scatter_dimension=0, tiled=True)]
    all_to_all x0 -> x1, starting transfers between devices: none -> 3.34 us  [dense(): lax.all_to_all(jnp.stack([gate_table(route_ids, route_gates, experts)] *...]
  transfers between devices with their start and end apart: 3 -> 4, of which waited for: 2 -> 4; matrix products, arithmetic and copies ran while one was open for 0% -> 0% of each run, Pallas kernels for 0% -> 0%
where the time goes in v1:
time: 253 us
  waiting for transfers between devices  213 us (84%)
  matrix products  19.5 us (8%)
  between operations  13.2 us (5%)
  starting transfers between devices  3.42 us (1%)
  other arithmetic  2.91 us (1%)
    reduce_scatter x1, waiting for transfers between devices, dense(): return lax.psum_scatter(out, 'ctx', scatter_dimension=0, tiled=True)  104 us
    all_gather x1, waiting for transfers between devices, dense(): rows = lax.all_gather(tokens, 'ctx', axis=0, tiled=True)  90.8 us
    dot_general x1, matrix products, expert_half(): gate_up = jnp.dot(rows, w_in[0], preferred_element_type=jnp.float32)  13.4 us
    psum x1, waiting for transfers between devices, expert_half(): summed = lax.psum(gate_up.astype(jnp.bfloat16), 'exp').astype(jnp.float32)  11.1 us
    all_to_all x1, waiting for transfers between devices, dense(): lax.all_to_all(jnp.stack([gate_table(route_ids, route_gates, experts)] *...  6.45 us
    dot_general x1, matrix products, expert_half(): jnp.dot(hidden, w_out[0], preferred_element_type=jnp.float32)  6.12 us
  transfers between devices with their start and end apart: 4, of which 4 were waited for; matrix products, arithmetic and copies ran while one was open for 0% of the time, Pallas kernels for 0%

profile of v1, /device:TPU:0, one launch (start us, length us, event | category | flops | bytes accessed | tf_op | source)
XLA Modules:
  0.0 253.3 jit_solution(2102381414069161173)
XLA Ops:
  6.5 0.0 all-gather.2.cloned.1.call-start
  6.5 0.7 all-gather.2.cloned.1.call-update
  7.3 0.0 copy-start
  7.3 0.0 copy-start.1
  7.3 0.0 all-reduce.2.cloned.1.call-start
  7.3 90.8 %all-gather.2.cloned.1.call-done = bf16[1024,2560]{1,0:T(8,128)(2,1)} async-done(((bf16[128,2560]{1,0:T(8,128)(2,1)}), bf16[1024,2560]{1,0:T(8,128)(2,1)}) %all-gather.2.cloned.1.call-update) | async-done | bytes 5242896 | tf_op jit(solution)/shard_map/all_gather | solution.py:32
  98.2 13.4 %fusion.3 = bf16[1024,1536]{1,0:T(8,128)(2,1)} fusion(bf16[1024,2560]{1,0:T(8,128)(2,1)} %all-gather.2.cloned.1.call-done, bf16[1,2560,1536]{2,1,0:T(8,128)(2,1)} %param.8), kind=kOutput, calls=%fused_computation.5 | convolution fusion | flops 8054636544 | bytes 16252928 | tf_op jit(solution)/shard_map/dot_general | solution.py:8
  111.6 0.0 all-reduce.2.cloned.1.call-update
  111.6 0.0 copy-done
  111.6 0.0 copy-done.1
  111.6 0.6 stack.2
  112.2 3.3 %all-to-all-start = ((f32[8,128,4]{1,2,0:T(4,128)}), f32[8,128,4]{1,2,0:T(4,128)S(1)}, u32[]{:S(2)}, u32[]{:S(2)}) async-start(f32[8,128,4]{1,2,0:T(4,128)} %stack.2), calls=%async_computation | async-start | bytes 32768 | tf_op jit(solution)/shard_map/all_to_all | solution.py:23
  115.6 0.0 reduce-scatter.2.cloned.1.call-start
  115.7 6.4 %all-to-all-done = f32[8,128,4]{1,2,0:T(4,128)S(1)} async-done(((f32[8,128,4]{1,2,0:T(4,128)}), f32[8,128,4]{1,2,0:T(4,128)S(1)}, u32[]{:S(2)}, u32[]{:S(2)}) %all-to-all-start) | async-done | bytes 16416 | tf_op jit(solution)/shard_map/all_to_all | solution.py:23
  122.1 11.1 %all-reduce.2.cloned.1.call-done = bf16[1024,1536]{1,0:T(8,128)(2,1)} async-done(((bf16[1024,1536]{1,0:T(8,128)(2,1)}), bf16[1024,1536]{1,0:T(8,128)(2,1)}) %all-reduce.2.cloned.1.call-update) | async-done | bytes 3145744 | tf_op jit(solution)/shard_map/psum | solution.py:9
  133.3 0.0 copy-start.2
  133.3 2.9 %convert_element_type.19 = f32[1024,1536]{1,0:T(8,128)S(1)} convert(bf16[1024,1536]{1,0:T(8,128)(2,1)} %all-reduce.2.cloned.1.call-done) | non-fusion elementwise | flops 1572864 | bytes 9437184 | tf_op jit(solution)/shard_map/convert_element_type | solution.py:9
  136.2 0.1 copy-done.2
  136.3 6.1 %multiply_convert_fusion = bf16[1024,2560]{1,0:T(8,128)(2,1)} fusion(f32[1024]{0:T(1024)S(1)} %bitcast.12, bf16[1,768,2560]{2,1,0:T(8,128)(2,1)S(1)} %copy-done.2, f32[1024,1536]{1,0:T(8,128)S(1)} %convert_element_type.19), kind=kOutput, calls=%fused_computation | convolution fusion | flops 4041736192 | bytes 15470592 | tf_op jit(solution)/shard_map/dot_general | solution.py:12
  142.4 0.0 reduce-scatter.2.cloned.1.call-update
  142.5 104.3 %reduce-scatter.2.cloned.1.call-done = bf16[128,2560]{1,0:T(8,128)(2,1)} async-done(((bf16[1024,2560]{1,0:T(8,128)(2,1)}), bf16[128,2560]{1,0:T(8,128)(2,1)}) %reduce-scatter.2.cloned.1.call-update) | async-done | bytes 655376 | tf_op jit(solution)/shard_map/reduce_scatter | solution.py:34
  (2 shorter events, 0.0 us)
Async XLA Ops:
  6.5 91.6 %all-gather.2.cloned.1.call-start = ((), (), s32[]{:S(2)}) async-start(), calls=%async_computation.2 | async-start | bytes 5898240 | tf_op jit(solution)/shard_map/all_gather | solution.py:32
  7.3 104.3 %copy-start = (f32[128,2]{0,1:T(2,128)S(1)}, f32[128,2]{0,1:T(2,128)}, u32[]{:S(2)}) copy-start(f32[128,2]{0,1:T(2,128)} %param.7) | copy-start | bytes 3076
  7.3 104.3 %copy-start.1 = (s32[128,2]{0,1:T(2,128)S(1)}, s32[128,2]{0,1:T(2,128)}, u32[]{:S(2)}) copy-start(s32[128,2]{0,1:T(2,128)} %param.6) | copy-start | bytes 3076
  7.3 126.0 %all-reduce.2.cloned.1.call-start = ((), (), s32[]{:S(2)}) async-start(), calls=%async_computation.3 | async-start | bytes 6291456 | tf_op jit(solution)/shard_map/psum | solution.py:9
  112.2 9.9 %all-to-all-start = ((f32[8,128,4]{1,2,0:T(4,128)}), f32[8,128,4]{1,2,0:T(4,128)S(1)}, u32[]{:S(2)}, u32[]{:S(2)}) async-start(f32[8,128,4]{1,2,0:T(4,128)} %stack.2), calls=%async_computation | async-start | bytes 32768 | tf_op jit(solution)/shard_map/all_to_all | solution.py:23
  115.6 131.2 %reduce-scatter.2.cloned.1.call-start = ((), (), s32[]{:S(2)}) async-start(), calls=%async_computation.4 | async-start | bytes 5898240 | tf_op jit(solution)/shard_map/reduce_scatter | solution.py:34
  133.3 3.1 %copy-start.2 = (bf16[1,768,2560]{2,1,0:T(8,128)(2,1)S(1)}, bf16[1,768,2560]{2,1,0:T(8,128)(2,1)}, u32[]{:S(2)}) copy-start(bf16[1,768,2560]{2,1,0:T(8,128)(2,1)} %param.9) | copy-start | bytes 11796484
Sparse Core Ops, SparseCore 0:
  9.5 88.5 all-gather.1
  111.7 21.4 all-reduce.1
  142.6 104.1 reduce-scatter.1
